TPU v7x, 32 devices: a whole 2x2x4 slice. The times are simulated.
32 devices in a mesh: seq: 8 (over y, x, core), wsh: 4 (over z).
Axes of the slice: x: 2, y: 2, z: 4, core: 2. Of those that a mesh axis runs over, the one named last changes fastest.
Arguments:
- x_in: bfloat16 [4, 4096, 1024], P('wsh', 'seq'), may hold values from -6 to 6
- seg_ids: int32 [4, 4096], P('wsh', 'seq'), may hold values from 0 to 7, never falling along the last dimension, each value on 1 to 2048 neighbouring positions
- in_weight: bfloat16 [1024, 4384], P('wsh'), may hold values from -0.1875 to 0.1875
- out_weight: bfloat16 [2048, 1024], P('wsh'), may hold values from -0.125 to 0.125
- conv_weight: bfloat16 [4, 2304], P(None, 'wsh'), may hold values from -3 to 3
- conv_bias: bfloat16 [2304], P('wsh'), may hold values from -0.5 to 0.5
- dt_bias: bfloat16 [32], P('wsh'), may hold values from -6 to -3
- a_log: bfloat16 [32], P('wsh'), may hold values from -4 to 1.5
- skip_gain: bfloat16 [32], P('wsh'), may hold values from 0.5 to 1.5
- norm_gain: bfloat16 [1024], P('wsh'), may hold values from 0.5 to 1.5
- gate_gain: bfloat16 [2048], P('wsh'), may hold values from 0.5 to 1.5
- cotangent: bfloat16 [4, 4096, 1024], P('wsh', 'seq'), may hold values from -6 to 6
Outputs:
- output: bfloat16 [4, 4096, 1024], P('wsh', 'seq')
- grad_input: float32 [4, 4096, 1024], P('wsh', 'seq')
- grad_in_weight: float32 [1024, 4384], P('wsh')
- grad_out_weight: float32 [2048, 1024], P('wsh')
- grad_conv_weight: float32 [4, 2304], P(None, 'wsh')
- grad_conv_bias: float32 [2304], P('wsh')
- grad_dt_bias: float32 [32], P('wsh')
- grad_a_log: float32 [32], P('wsh')
- grad_skip: float32 [32], P('wsh')
- grad_norm_gain: float32 [1024], P('wsh')
- grad_gate_gain: float32 [2048], P('wsh')
Inputs may be any that keep to these rules, and one draw needn't show every extreme that they name: `seg_ids`: in each stream, document numbers never fall, each document has 1 to 2048 rows and one has exactly 2048.
All inputs are finite; a program needn't handle non-finite values.
Results may differ from a plain program's by a relative error of at most 0.012.
The roundings to bfloat16 on the way count: a program that leaves them out, or rounds other values in their place, can miss the bound.
Values may be sent and summed in bfloat16 or wider, within the bound.
No kernel may reach another device: no remote copies, remote signals or barrier semaphores. Data moves between devices by JAX's collectives and lax.ppermute only.
A program may use at most 192 MiB of HBM per device.

v0:
```python
import jax
import jax.numpy as jnp
from jax import lax
from jax.sharding import PartitionSpec as P

BLOCK = 512
epsilon = 1e-05
highest = lax.Precision.HIGHEST


def shifted(value, axis, steps):
    count = lax.axis_size(axis)
    first, last = (max(0, -steps), min(count, count - steps))
    return lax.ppermute(value, axis, [(source, source + steps) for source in range(first, last)])


def rms_scale(values, gain_vec):
    return (
        values * lax.rsqrt(jnp.mean(values * values, axis=-1, keepdims=True) + epsilon) * gain_vec
    )


def gated_norm(scanned, gate_part, gain_vec):
    return rms_scale(scanned * jax.nn.silu(gate_part), gain_vec)


def conv_silu(extended, ext_ids, conv_weight, conv_bias):
    tap_count = conv_weight.shape[0]
    rows_count = extended.shape[0] - tap_count + 1
    current = ext_ids[tap_count - 1 :]
    summed = jnp.zeros((rows_count, extended.shape[1]), jnp.float32) + conv_bias[None, :]
    for offset in range(tap_count):
        window = extended[offset : offset + rows_count]
        matching = (ext_ids[offset : offset + rows_count] == current).astype(jnp.float32)
        summed = summed + window * conv_weight[offset][None, :] * matching[:, None]
    return jax.nn.silu(summed)


def scan_heads(head_x, head_dt, b_rows, c_rows, segment_ids, dt_bias, a_log, skip_gain, block_rows):
    length = head_x.shape[0]
    head_count = head_dt.shape[1]
    head_dim = head_x.shape[1] // head_count
    state_dim = b_rows.shape[1]
    blocks = length // block_rows
    step_size = jax.nn.softplus(head_dt + dt_bias[None, :])
    log_decay = -jnp.exp(a_log)[None, :] * step_size
    x_heads = head_x.reshape(length, head_count, head_dim)
    scaled = x_heads * step_size[:, :, None]
    prev_ids = jnp.concatenate(
        [jnp.full((1,), -1, jnp.int32), segment_ids[block_rows - 1 :: block_rows][:-1]]
    )
    lower_mask = jnp.tril(jnp.ones((block_rows, block_rows), jnp.bool_))

    def one_block(carry_state, pieces):
        decay_part, scaled_part, b_part, c_part, id_part, prev_id = pieces
        cumulative = jnp.cumsum(decay_part, axis=0)
        linked = (id_part[:, None] == id_part[None, :]) & lower_mask
        differ = cumulative.T[:, :, None] - cumulative.T[:, None, :]
        kernel = jnp.where(linked[None], jnp.exp(jnp.where(linked[None], differ, 0.0)), 0.0)
        scores = jnp.dot(c_part, b_part.T, precision=highest)
        mixed_kernel = kernel * scores[None]
        intra_out = jnp.einsum("hts,shp->thp", mixed_kernel, scaled_part, precision=highest)
        carried = (id_part == prev_id).astype(jnp.float32)
        carry_in = jnp.exp(cumulative) * carried[:, None]
        inter_out = (
            jnp.einsum("tn,hpn->thp", c_part, carry_state, precision=highest) * carry_in[:, :, None]
        )
        end_link = (id_part == id_part[-1]).astype(jnp.float32)
        to_end = jnp.exp(cumulative[-1][None, :] - cumulative) * end_link[:, None]
        fresh = jnp.einsum(
            "shp,sn->hpn", to_end[:, :, None] * scaled_part, b_part, precision=highest
        )
        block_decay = jnp.exp(cumulative[-1]) * carried[-1]
        new_state = carry_state * block_decay[:, None, None] + fresh
        return (new_state, intra_out + inter_out)

    pieces = (
        log_decay.reshape(blocks, block_rows, head_count),
        scaled.reshape(blocks, block_rows, head_count, head_dim),
        b_rows.reshape(blocks, block_rows, state_dim),
        c_rows.reshape(blocks, block_rows, state_dim),
        segment_ids.reshape(blocks, block_rows),
        prev_ids,
    )
    initial = jnp.zeros((head_count, head_dim, state_dim), jnp.float32)
    ignored, outputs = lax.scan(jax.checkpoint(one_block), initial, pieces)
    result = outputs.reshape(length, head_count, head_dim) + skip_gain[None, :, None] * x_heads
    return result.reshape(length, head_count * head_dim)


def local(
    x_in,
    seg_ids,
    in_weight,
    out_weight,
    conv_weight,
    conv_bias,
    dt_bias,
    a_log,
    skip_gain,
    norm_gain,
    gate_gain,
    cotangent,
):
    w_in, w_out, conv_full, bias_full, dt_full, alog_full, skip_full, norm_full, gate_full = (
        lax.all_gather(in_weight, "wsh", axis=0, tiled=True),
        lax.all_gather(out_weight, "wsh", axis=0, tiled=True),
        lax.all_gather(conv_weight, "wsh", axis=1, tiled=True),
        lax.all_gather(conv_bias, "wsh", axis=0, tiled=True),
        lax.all_gather(dt_bias, "wsh", axis=0, tiled=True),
        lax.all_gather(a_log, "wsh", axis=0, tiled=True),
        lax.all_gather(skip_gain, "wsh", axis=0, tiled=True),
        lax.all_gather(norm_gain, "wsh", axis=0, tiled=True),
        lax.all_gather(gate_gain, "wsh", axis=0, tiled=True),
    )
    tok_rows = x_in.shape[1]
    seq_count = lax.axis_size("seq")
    seq_index = lax.axis_index("seq")
    row_start = seq_index * tok_rows
    inner_width = w_out.shape[0]
    head_count = dt_full.shape[0]
    state_dim = (w_in.shape[1] - 2 * inner_width - head_count) // 2
    channels = inner_width + 2 * state_dim
    tap_count = conv_full.shape[0]
    residual_in = x_in[0].astype(jnp.float32)
    ids_full = lax.all_gather(seg_ids, "seq", axis=1, tiled=True)[0]
    normed_f, norm_pull = jax.vjp(rms_scale, residual_in, norm_full.astype(jnp.float32))
    normed = normed_f.astype(jnp.bfloat16)
    projected = jnp.dot(normed, w_in, preferred_element_type=jnp.float32).astype(jnp.bfloat16)
    gate_part = projected[:, :inner_width]
    conv_in = projected[:, inner_width : inner_width + channels]
    dt_part = projected[:, inner_width + channels :]
    halo_rows = shifted(conv_in[tok_rows - (tap_count - 1) :], "seq", 1)
    extended = jnp.concatenate([halo_rows, conv_in]).astype(jnp.float32)
    padded_ids = jnp.concatenate([jnp.full((tap_count - 1,), -1, jnp.int32), ids_full])
    ext_ids = lax.dynamic_slice_in_dim(padded_ids, row_start, tok_rows + tap_count - 1)

    def conv_local(ext_rows, weights, biases):
        return conv_silu(ext_rows, ext_ids, weights, biases)

    activated, conv_pull = jax.vjp(
        conv_local, extended, conv_full.astype(jnp.float32), bias_full.astype(jnp.float32)
    )
    x_part = activated[:, :inner_width].astype(jnp.bfloat16)
    bc_part = activated[:, inner_width:].astype(jnp.bfloat16)
    head_x, head_dt = (
        lax.all_to_all(x_part, "seq", split_axis=1, concat_axis=0, tiled=True),
        lax.all_to_all(dt_part, "seq", split_axis=1, concat_axis=0, tiled=True),
    )
    bc_full = lax.all_gather(bc_part, "seq", axis=0, tiled=True)
    local_heads = head_count // seq_count
    head_start = seq_index * local_heads
    dt_local = lax.dynamic_slice_in_dim(dt_full, head_start, local_heads).astype(jnp.float32)
    alog_local = lax.dynamic_slice_in_dim(alog_full, head_start, local_heads).astype(jnp.float32)
    skip_local = lax.dynamic_slice_in_dim(skip_full, head_start, local_heads).astype(jnp.float32)

    def scan_local(x_vals, dt_vals, b_vals, c_vals, bias_vals, decay_vals, skip_vals):
        return scan_heads(
            x_vals, dt_vals, b_vals, c_vals, ids_full, bias_vals, decay_vals, skip_vals, BLOCK
        )

    scanned, scan_pull = jax.vjp(
        scan_local,
        head_x.astype(jnp.float32),
        head_dt.astype(jnp.float32),
        bc_full[:, :state_dim].astype(jnp.float32),
        bc_full[:, state_dim:].astype(jnp.float32),
        dt_local,
        alog_local,
        skip_local,
    )
    y_rows = lax.all_to_all(
        scanned.astype(jnp.bfloat16), "seq", split_axis=0, concat_axis=1, tiled=True
    )
    gated_f, gated_pull = jax.vjp(
        gated_norm,
        y_rows.astype(jnp.float32),
        gate_part.astype(jnp.float32),
        gate_full.astype(jnp.float32),
    )
    gated = gated_f.astype(jnp.bfloat16)
    output = (residual_in + jnp.dot(gated, w_out, preferred_element_type=jnp.float32)).astype(
        jnp.bfloat16
    )
    grad_out = cotangent[0]
    grad_wout = lax.dot_general(
        gated, grad_out, (((0,), (0,)), ((), ())), preferred_element_type=jnp.float32
    )
    grad_gated = lax.dot_general(
        grad_out, w_out, (((1,), (1,)), ((), ())), preferred_element_type=jnp.float32
    )
    grad_y, grad_gate_part, grad_gate_gain = gated_pull(grad_gated)
    head_grad = lax.all_to_all(
        grad_y.astype(jnp.bfloat16), "seq", split_axis=1, concat_axis=0, tiled=True
    )
    grad_hx, grad_hdt, grad_b, grad_c, grad_bias, grad_decay, grad_skipped = scan_pull(
        head_grad.astype(jnp.float32)
    )
    back_x, back_dt = (
        lax.all_to_all(
            grad_hx.astype(jnp.bfloat16), "seq", split_axis=0, concat_axis=1, tiled=True
        ),
        lax.all_to_all(
            grad_hdt.astype(jnp.bfloat16), "seq", split_axis=0, concat_axis=1, tiled=True
        ),
    )
    grad_bc = lax.psum_scatter(
        jnp.concatenate([grad_b, grad_c], axis=1).astype(jnp.bfloat16),
        "seq",
        scatter_dimension=0,
        tiled=True,
    ).astype(jnp.float32)
    grad_act = jnp.concatenate([back_x.astype(jnp.float32), grad_bc], axis=1)
    grad_ext, grad_convw, grad_convb = conv_pull(grad_act)
    rim_back = shifted(grad_ext[: tap_count - 1], "seq", -1)
    grad_conv_in = jnp.concatenate(
        [grad_ext[tap_count - 1 : tok_rows], grad_ext[tok_rows:] + rim_back]
    )
    grad_proj = jnp.concatenate(
        [grad_gate_part, grad_conv_in, back_dt.astype(jnp.float32)], axis=1
    ).astype(jnp.bfloat16)
    grad_win = lax.dot_general(
        normed, grad_proj, (((0,), (0,)), ((), ())), preferred_element_type=jnp.float32
    )
    grad_normed = lax.dot_general(
        grad_proj, w_in, (((1,), (1,)), ((), ())), preferred_element_type=jnp.float32
    )
    grad_resid, grad_norm = norm_pull(grad_normed)
    grad_input = grad_resid + grad_out.astype(jnp.float32)

    def place_heads(values):
        return lax.dynamic_update_slice_in_dim(
            jnp.zeros((head_count,), jnp.float32), values, head_start, 0
        )

    grad_dtb = place_heads(grad_bias)
    grad_alog = place_heads(grad_decay)
    grad_skip = place_heads(grad_skipped)
    summed = lax.psum(
        (
            grad_win,
            grad_wout,
            grad_convw,
            grad_convb,
            grad_dtb,
            grad_alog,
            grad_skip,
            grad_norm,
            grad_gate_gain,
        ),
        "seq",
    )
    shards = (
        lax.psum_scatter(summed[0], "wsh", scatter_dimension=0, tiled=True),
        lax.psum_scatter(summed[1], "wsh", scatter_dimension=0, tiled=True),
        lax.psum_scatter(summed[2], "wsh", scatter_dimension=1, tiled=True),
        lax.psum_scatter(summed[3], "wsh", scatter_dimension=0, tiled=True),
        lax.psum_scatter(summed[4], "wsh", scatter_dimension=0, tiled=True),
        lax.psum_scatter(summed[5], "wsh", scatter_dimension=0, tiled=True),
        lax.psum_scatter(summed[6], "wsh", scatter_dimension=0, tiled=True),
        lax.psum_scatter(summed[7], "wsh", scatter_dimension=0, tiled=True),
        lax.psum_scatter(summed[8], "wsh", scatter_dimension=0, tiled=True),
    )
    return (
        output[None],
        grad_input[None],
        shards[0],
        shards[1],
        shards[2],
        shards[3],
        shards[4],
        shards[5],
        shards[6],
        shards[7],
        shards[8],
    )


def solution(mesh):
    in_specs = (
        P("wsh", "seq", None),
        P("wsh", "seq"),
        P("wsh", None),
        P("wsh", None),
        P(None, "wsh"),
        P("wsh"),
        P("wsh"),
        P("wsh"),
        P("wsh"),
        P("wsh"),
        P("wsh"),
        P("wsh", "seq", None),
    )
    out_specs = (
        P("wsh", "seq", None),
        P("wsh", "seq", None),
        P("wsh", None),
        P("wsh", None),
        P(None, "wsh"),
        P("wsh"),
        P("wsh"),
        P("wsh"),
        P("wsh"),
        P("wsh"),
        P("wsh"),
    )
    return jax.shard_map(local, mesh=mesh, in_specs=in_specs, out_specs=out_specs, check_vma=False)
```

profile of v0, /device:TPU:0, one launch (start us, length us, event | category | flops | bytes accessed | tf_op | source)
XLA Modules:
  0.0 1654.8 jit_solution(10845675449132418567)
XLA Ops:
  8.6 12.6 all-gather
  21.3 31.8 %all-gather.1 = bf16[4,576,4]{1,2,0:T(4,128)(2,1)S(1)} all-gather(bf16[1,576,4]{1,2,0:T(4,128)(2,1)} %bitcast.442), channel_id=1, replica_groups=mesh['seq'=8,'wsh'=4] {'wsh'}, dimensions={0}, use_global_device_ids=true | all-gather | bytes 23040 | tf_op jit(solution)/shard_map/all_gather | solution.py:108
  63.9 107.3 %all-gather.7.cloned.1.call-done = bf16[1024,4384]{0,1:T(8,128)(2,1)} async-done(((bf16[256,4384]{0,1:T(8,128)(2,1)}), bf16[1024,4384]{0,1:T(8,128)(2,1)}) %all-gather.7.cloned.1.call-update) | async-done | bytes 8978448 | tf_op jit(solution)/shard_map/all_gather | solution.py:106
  222.2 27.8 %all-to-all-done.1 = bf16[512,8,256]{0,2,1:T(8,128)(2,1)S(1)} async-done(((bf16[512,8,256]{0,2,1:T(8,128)(2,1)}), bf16[512,8,256]{0,2,1:T(8,128)(2,1)S(1)}, u32[]{:S(2)}, u32[]{:S(2)}) %all-to-all-start.1) | async-done | bytes 2097184 | tf_op jit(solution)/shard_map/all_to_all | solution.py:147
  262.3 271.7 %while.40 = (s32[]{:T(128)}, f32[4,64,128]{2,1,0:T(8,128)S(1)}, f32[8,512,4,64]{1,0,3,2:T(8,128)}, f32[8,4,64,128]{3,2,1,0:T(8,128)}, f32[8,512,4]{1,2,0:T(4,128...) while((s32[]{:T(128)}, f32[4,64,128]{2,1,0:T(8,128)S(1)}, ...), condition=%wide.region_4.5_spmd.clone, body=%wide.region_1.4_spmd.clone.sunk | while | flops 1616420864 | bytes 9202848 | solution.py:86
  284.8 11.5 dynamic_update_slice.83
  318.8 11.5 dynamic_update_slice.83
  352.7 11.5 dynamic_update_slice.83
  386.7 11.5 dynamic_update_slice.83
  420.6 11.5 dynamic_update_slice.83
  488.5 11.5 dynamic_update_slice.83
  522.5 11.5 dynamic_update_slice.83
  543.2 11.9 all-gather.2
  555.1 14.6 all-to-all-done.2
  603.2 26.5 %all-to-all-done.3 = bf16[512,8,256]{0,2,1:T(8,128)(2,1)S(1)} async-done(((bf16[512,8,256]{0,2,1:T(8,128)(2,1)}), bf16[512,8,256]{0,2,1:T(8,128)(2,1)S(1)}, u32[]{:S(2)}, u32[]{:S(2)}) %all-to-all-start.3) | async-done | bytes 2097184 | tf_op jit(solution)/shard_map/all_to_all | solution.py:193
  638.3 369.4 %while.41 = (s32[]{:T(128)}, f32[4,64,128]{2,1,0:T(8,128)S(1)}, f32[8,512,4]{1,2,0:T(4,128)}, f32[8,512,4,64]{1,3,2,0:T(8,128)}, bf16[8,512,128]{2,1,0:T(8,128)(...) while((s32[]{:T(128)}, f32[4,64,128]{2,1,0:T(8,128)S(1)}, ...), condition=%wide.region_19.20_spmd.clone, body=%wide.region_7.19_spmd.clone.sunk | while | flops 3843487744 | bytes 28192232 | solution.py:86
  1050.1 26.4 %all-to-all-done.4 = bf16[8,512,256]{1,2,0:T(8,128)(2,1)} async-done(((bf16[8,512,256]{1,2,0:T(8,128)(2,1)}), bf16[8,512,256]{1,2,0:T(8,128)(2,1)}, u32[]{:S(2)}, u32[]{:S(2)}) %all-to-all-start.4) | async-done | bytes 2097184 | tf_op jit(solution)/shard_map/all_to_all | solution.py:200
  1080.5 12.2 multiply_reduce_fusion.6
  1115.9 80.4 %reduce-scatter.11.cloned.1.call-done = f32[512,1024]{1,0:T(8,128)} async-done(((f32[2048,1024]{1,0:T(8,128)}), f32[512,1024]{1,0:T(8,128)}) %reduce-scatter.11.cloned.1.call-update) | async-done | bytes 2097168 | tf_op jit(solution)/shard_map/reduce_scatter | solution.py:255
  1196.3 302.1 %reduce-scatter.9.cloned.1.call-done = f32[256,4384]{0,1:T(8,128)} async-done(((f32[1024,4384]{0,1:T(8,128)}), f32[256,4384]{0,1:T(8,128)}) %reduce-scatter.9.cloned.1.call-update) | async-done | bytes 4489232 | tf_op jit(solution)/shard_map/reduce_scatter | solution.py:254
  1510.0 11.8 fusion.107
  1521.8 18.7 %all-reduce.23 = (f32[2304]{0:T(1024)S(1)}, f32[32]{0:T(128)S(1)}, f32[32]{0:T(128)S(1)}, f32[32]{0:T(128)S(1)}, f32[1024]{0:T(1024)S(1)}, /*index=5*/f32[2048]{0:T(1024)S(1)}) all-reduce(f32[2304]{0:T(1024)S(1)} %get-tuple-element.698, f32[32]{0:T(128)S(1)} %dynamic_update_slice.61, ...), channel_id=6, replica_groups=mesh['seq'=8,'wsh'=4] {'wsh'}, use_global_device_ids=true, to_apply=%region_35.36.clone | all-reduce | flops 5472 | bytes 43776
  1545.6 24.4 %all-reduce.21 = (f32[4,576]{1,0:T(4,128)}, f32[576]{0:T(1024)}, f32[8]{0:T(128)}, f32[8]{0:T(128)}, f32[8]{0:T(128)}, /*index=5*/f32[256]{0:T(256)}, f32[512]{0:T(512)}) all-reduce(f32[4,576]{1,0:T(4,128)S(1)} %copy.188, f32[576]{0:T(1024)S(1)} %dynamic-slice.5, f32[8]{0:T(128)S(1)} %dynamic-slice.7, ...), channel_id=1, replica_groups=mesh['seq'=8,'wsh'=4] {'seq'}, use_global_device_ids=true, to_apply=%region_31.32 | all-reduce | flops 3672 | bytes 29376 | tf_op jit(solution)/shard_map/psum | solution.py:239
  1570.0 71.6 %all-reduce.27.cloned.1.call-done = (f32[256,4384]{0,1:T(8,128)}, f32[512,1024]{1,0:T(8,128)}) async-done(((f32[256,4384]{0,1:T(8,128)}, f32[512,1024]{1,0:T(8,128)}), (f32[256,4384]{0,1:T(8,128)}, f32[512,1024]{1,0:T(8,128)})) %all-reduce.27.cloned.1.call-update) | async-done | bytes 6586384 | tf_op jit(solution)/shard_map/psum | solution.py:239
  (867 shorter events, 772.7 us)
Async XLA Ops:
  7.2 164.1 %all-gather.7.cloned.1.call-start = ((), (), s32[]{:S(2)}) async-start(), calls=%async_computation.10 | async-start | bytes 11223040 | tf_op jit(solution)/shard_map/all_gather | solution.py:106
  7.9 249.8 %all-gather.9.cloned.1.call-start = ((), (), s32[]{:S(2)}) async-start(), calls=%async_computation.11 | async-start | bytes 2359296 | tf_op jit(solution)/shard_map/all_gather | solution.py:150
  21.3 159.2 %copy-start.47 = (f32[4,1,256]{2,1,0:T(1,128)}, f32[4,1,256]{2,1,0:T(1,128)S(1)}, u32[]{:S(2)}) copy-start(f32[4,1,256]{2,1,0:T(1,128)S(1)} %convert_element_type.252) | copy-start | bytes 12292
  63.8 116.7 %copy-start.45 = (f32[512]{0:T(512)}, f32[512]{0:T(512)S(1)}, u32[]{:S(2)}) copy-start(f32[512]{0:T(512)S(1)} %fusion.110) | copy-start | bytes 6148
  63.8 116.7 %copy-start.51 = (f32[512]{0:T(512)}, f32[512]{0:T(512)S(1)}, u32[]{:S(2)}) copy-start(f32[512]{0:T(512)S(1)} %fusion.134) | copy-start | bytes 6148
  63.9 133.4 %copy-start.37 = (f32[512]{0:T(512)}, f32[512]{0:T(512)S(1)}, u32[]{:S(2)}) copy-start(f32[512]{0:T(512)S(1)} %get-tuple-element.812) | copy-start | bytes 6148
  63.9 133.5 %copy-start.39 = (f32[512]{0:T(512)}, f32[512]{0:T(512)S(1)}, u32[]{:S(2)}) copy-start(f32[512]{0:T(512)S(1)} %get-tuple-element.813) | copy-start | bytes 6148
  63.9 133.5 %copy-start.41 = (f32[512]{0:T(512)}, f32[512]{0:T(512)S(1)}, u32[]{:S(2)}) copy-start(f32[512]{0:T(512)S(1)} %get-tuple-element.814) | copy-start | bytes 6148
  182.8 14.0 collective-permute-start
  204.3 9.4 all-to-all-start
  213.6 36.4 %all-to-all-start.1 = ((bf16[512,8,256]{0,2,1:T(8,128)(2,1)}), bf16[512,8,256]{0,2,1:T(8,128)(2,1)S(1)}, u32[]{:S(2)}, u32[]{:S(2)}) async-start(bf16[512,8,256]{0,2,1:T(8,128)(2,1)} %bitcast.407), calls=%async_computation.1 | async-start | bytes 4194304 | tf_op jit(solution)/shard_map/all_to_all | solution.py:147
  217.8 366.5 %all-gather.11.cloned.1.call-start = ((), (), s32[]{:S(2)}) async-start(), calls=%async_computation.12 | async-start | bytes 5242880 | tf_op jit(solution)/shard_map/all_gather | solution.py:107
  220.7 313.3 %copy-start.49 = (f32[256]{0:T(256)}, f32[256]{0:T(256)S(1)}, u32[]{:S(2)}) copy-start(f32[256]{0:T(256)S(1)} %mul.804) | copy-start | bytes 3076
  250.0 284.0 %copy-start.6 = (bf16[512,8,256]{0,2,1:T(8,128)(2,1)}, bf16[512,8,256]{0,2,1:T(8,128)(2,1)S(1)}, u32[]{:S(2)}) copy-start(bf16[512,8,256]{0,2,1:T(8,128)(2,1)S(1)} %all-to-all-done.1) | copy-start | bytes 6291460
  539.5 30.2 %all-to-all-start.2 = ((bf16[8,512,256]{1,2,0:T(8,128)(2,1)}), bf16[8,512,256]{1,2,0:T(8,128)(2,1)S(1)}, u32[]{:S(2)}, u32[]{:S(2)}) async-start(bf16[8,512,256]{1,2,0:T(8,128)(2,1)} %copy.172), calls=%async_computation.2 | async-start | bytes 4194304 | tf_op jit(solution)/shard_map/all_to_all | solution.py:172
  599.5 30.2 %all-to-all-start.3 = ((bf16[512,8,256]{0,2,1:T(8,128)(2,1)}), bf16[512,8,256]{0,2,1:T(8,128)(2,1)S(1)}, u32[]{:S(2)}, u32[]{:S(2)}) async-start(bf16[512,8,256]{0,2,1:T(8,128)(2,1)} %bitcast.408), calls=%async_computation.3 | async-start | bytes 4194304 | tf_op jit(solution)/shard_map/all_to_all | solution.py:193
  603.1 477.3 %reduce-scatter.7.cloned.1.call-start = ((), (), s32[]{:S(2)}) async-start(), calls=%async_computation.13 | async-start | bytes 2359296 | tf_op jit(solution)/shard_map/reduce_scatter | solution.py:207
  1011.0 185.3 %reduce-scatter.11.cloned.1.call-start = ((), (), s32[]{:S(2)}) async-start(), calls=%async_computation.15 | async-start | bytes 10485760 | tf_op jit(solution)/shard_map/reduce_scatter | solution.py:255
  1034.6 10.9 all-to-all-start.5
  1045.5 31.0 %all-to-all-start.4 = ((bf16[8,512,256]{1,2,0:T(8,128)(2,1)}), bf16[8,512,256]{1,2,0:T(8,128)(2,1)}, u32[]{:S(2)}, u32[]{:S(2)}) async-start(bf16[8,512,256]{1,2,0:T(8,128)(2,1)} %copy.178), calls=%async_computation.4 | async-start | bytes 4194304 | tf_op jit(solution)/shard_map/all_to_all | solution.py:200
  1049.9 448.5 %reduce-scatter.9.cloned.1.call-start = ((), (), s32[]{:S(2)}) async-start(), calls=%async_computation.14 | async-start | bytes 22446080 | tf_op jit(solution)/shard_map/reduce_scatter | solution.py:254
  1094.6 4.0 collective-permute-start.1
  1111.7 432.8 %reduce-scatter.13.cloned.1.call-start = ((), (), s32[]{:S(2)}) async-start(), calls=%async_computation.16 | async-start | bytes 1474560
  1113.3 528.3 %all-reduce.27.cloned.1.call-start = ((), (), s32[]{:S(2)}) async-start(), calls=%async_computation.17 | async-start | bytes 13172736 | tf_op jit(solution)/shard_map/psum | solution.py:239
  (88 other events, 941.6 us)
Sparse Core Ops, SparseCore 0:
  9.5 161.6 all-gather.6
  203.7 38.2 all-gather.8
  243.6 79.8 all-gather.10
  1011.1 38.2 reduce-scatter.6
  1051.6 144.6 reduce-scatter.10
  1198.5 299.8 reduce-scatter.8
  1500.7 30.4 reduce-scatter.12
  1534.7 106.8 all-reduce.26
where the time goes:
time: 1670 us; the launch traced here: 1650 us
  waiting for transfers between devices  658 us (39%)
  matrix products  320 us (19%)
  local copies, waits for them, and re-layouts  300 us (18%)
  other arithmetic  211 us (13%)
  blocking collectives  118 us (7%)
  starting transfers between devices  26.4 us (2%)
  between operations  19.3 us (1%)
    reduce_scatter x1, waiting for transfers between devices, local(): lax.psum_scatter(summed[0], 'wsh', scatter_dimension=0, tiled=True)  302 us
    dot_general x24, matrix products, one_block(): jnp.einsum('hts,shp->thp', mixed_kernel, scaled_part, precision=highest)  145 us
    all_gather x1, waiting for transfers between devices, local(): lax.all_gather(in_weight, 'wsh', axis=0, tiled=True)  107 us
    dynamic_update_slice x24, local copies, waits for them, and re-layouts, scan_heads(): ignored, outputs = lax.scan(jax.checkpoint(one_block), initial, pieces)  101 us
    another operation x60, other arithmetic  90.8 us
    reduce_scatter x1, waiting for transfers between devices, local(): lax.psum_scatter(summed[1], 'wsh', scatter_dimension=0, tiled=True)  80.4 us
    psum x1, waiting for transfers between devices, local(): lax.psum((grad_win, grad_wout, grad_convw, grad_convb, grad_dtb, grad_alo...  71.6 us
    dot_general x32, matrix products, one_block(): scores = jnp.dot(c_part, b_part.T, precision=highest)  64.9 us
  transfers between devices with their start and end apart: 16, of which 8 were waited for; matrix products, arithmetic and copies ran while one was open for 25% of the time, Pallas kernels for 0%

commit v1 on v0

--- a/solution.py
+++ b/solution.py
@@ -144,7 +144,10 @@
     x_part = activated[:, :inner_width].astype(jnp.bfloat16)
     bc_part = activated[:, inner_width:].astype(jnp.bfloat16)
     head_x, head_dt = (
-        lax.all_to_all(x_part, "seq", split_axis=1, concat_axis=0, tiled=True),
+        jnp.concatenate(
+            lax.all_to_all(jnp.stack(jnp.split(x_part, lax.axis_size("seq"), axis=1)), "seq", 0, 0),
+            axis=0,
+        ),
         lax.all_to_all(dt_part, "seq", split_axis=1, concat_axis=0, tiled=True),
     )
     bc_full = lax.all_gather(bc_part, "seq", axis=0, tiled=True)

time: 1670 us -> 1520 us (0.910)
  local copies, waits for them, and re-layouts: 300 us -> 158 us
    dynamic_update_slice x24 -> x8, local copies, waits for them, and re-layouts: 101 us -> 4.8 us  [scan_heads(): ignored, outputs = lax.scan(jax.checkpoint(one_block), initial, pieces)]
    dynamic_slice x40 -> x32, local copies, waits for them, and re-layouts: 52.8 us -> 9.72 us  [scan_heads(): ignored, outputs = lax.scan(jax.checkpoint(one_block), initial, pieces)]
    another operation x60 -> x59, other arithmetic: 90.8 us -> 91.4 us
  transfers between devices with their start and end apart: 16 -> 16, of which waited for: 8 -> 8; matrix products, arithmetic and copies ran while one was open for 25% -> 19% of each run, Pallas kernels for 0% -> 0%
where the time goes in v1:
time: 1520 us; the launch traced here: 1510 us
  waiting for transfers between devices  658 us (43%)
  matrix products  324 us (21%)
  other arithmetic  206 us (14%)
  local copies, waits for them, and re-layouts  158 us (10%)
  blocking collectives  119 us (8%)
  starting transfers between devices  26.4 us (2%)
  between operations  19.2 us (1%)
    reduce_scatter x1, waiting for transfers between devices, local(): lax.psum_scatter(summed[0], 'wsh', scatter_dimension=0, tiled=True)  302 us
    dot_general x24, matrix products, one_block(): jnp.einsum('hts,shp->thp', mixed_kernel, scaled_part, precision=highest)  149 us
    all_gather x1, waiting for transfers between devices, local(): lax.all_gather(in_weight, 'wsh', axis=0, tiled=True)  107 us
    another operation x59, other arithmetic  91.4 us
    reduce_scatter x1, waiting for transfers between devices, local(): lax.psum_scatter(summed[1], 'wsh', scatter_dimension=0, tiled=True)  78.7 us
    psum x1, waiting for transfers between devices, local(): lax.psum((grad_win, grad_wout, grad_convw, grad_convb, grad_dtb, grad_alo...  72.2 us
    dot_general x32, matrix products, one_block(): scores = jnp.dot(c_part, b_part.T, precision=highest)  56.9 us
    dot_general x32, matrix products, one_block(): jnp.einsum('tn,hpn->thp', c_part, carry_state, precision=highest)  37.7 us
  transfers between devices with their start and end apart: 16, of which 8 were waited for; matrix products, arithmetic and copies ran while one was open for 19% of the time, Pallas kernels for 0%

profile of v1, /device:TPU:0, one launch (start us, length us, event | category | flops | bytes accessed | tf_op | source)
XLA Modules:
  0.0 1512.7 jit_solution(9965487144411868096)
XLA Ops:
  8.6 12.6 all-gather
  21.3 31.8 %all-gather.1 = bf16[4,576,4]{1,2,0:T(4,128)(2,1)S(1)} all-gather(bf16[1,576,4]{1,2,0:T(4,128)(2,1)} %bitcast.476), channel_id=1, replica_groups=mesh['seq'=8,'wsh'=4] {'wsh'}, dimensions={0}, use_global_device_ids=true | all-gather | bytes 23040 | tf_op jit(solution)/shard_map/all_gather | solution.py:108
  53.2 9.0 all_gather.37
  64.5 106.8 %all-gather.7.cloned.1.call-done = bf16[1024,4384]{0,1:T(8,128)(2,1)} async-done(((bf16[256,4384]{0,1:T(8,128)(2,1)}), bf16[1024,4384]{0,1:T(8,128)(2,1)}) %all-gather.7.cloned.1.call-update) | async-done | bytes 8978448 | tf_op jit(solution)/shard_map/all_gather | solution.py:106
  171.3 9.3 convolution_convert_fusion
  187.3 9.5 all-reduce.24
  220.8 29.5 %all-to-all-done.1 = bf16[8,512,256]{2,1,0:T(8,128)(2,1)S(1)} async-done(((bf16[8,512,256]{2,1,0:T(8,128)(2,1)}), bf16[8,512,256]{2,1,0:T(8,128)(2,1)S(1)}, u32[]{:S(2)}, u32[]{:S(2)}) %all-to-all-start.1) | async-done | bytes 2097184 | tf_op jit(solution)/shard_map/all_to_all | solution.py:148
  265.6 157.4 %while.40 = (s32[]{:T(128)}, f32[4,64,128]{2,1,0:T(8,128)S(1)}, f32[8,512,4,64]{1,3,2,0:T(8,128)}, f32[8,4,64,128]{3,2,1,0:T(8,128)}, f32[8,512,4]{1,2,0:T(4,128...) while((s32[]{:T(128)}, f32[4,64,128]{2,1,0:T(8,128)S(1)}, ...), condition=%wide.region_4.5_spmd.clone, body=%wide.region_1.4_spmd.clone.sunk | while | flops 1616420864 | bytes 7107223 | solution.py:86
  289.9 6.8 fusion.216
  436.2 12.1 all-gather.2
  448.4 14.4 all-to-all-done.2
  469.6 7.0 multiply_reduce_fusion.7
  487.4 26.5 %all-to-all-done.3 = bf16[512,8,256]{2,0,1:T(8,128)(2,1)S(1)} async-done(((bf16[512,8,256]{2,0,1:T(8,128)(2,1)}), bf16[512,8,256]{2,0,1:T(8,128)(2,1)S(1)}, u32[]{:S(2)}, u32[]{:S(2)}) %all-to-all-start.3) | async-done | bytes 2097184 | tf_op jit(solution)/shard_map/all_to_all | solution.py:196
  527.3 338.0 %while.41 = (s32[]{:T(128)}, f32[4,64,128]{2,1,0:T(8,128)S(1)}, f32[8,512,4]{1,2,0:T(4,128)}, f32[8,512,4,64]{1,3,2,0:T(8,128)}, bf16[8,512,128]{2,1,0:T(8,128)(...) while((s32[]{:T(128)}, f32[4,64,128]{2,1,0:T(8,128)S(1)}, ...), condition=%wide.region_19.20_spmd.clone, body=%wide.region_7.19_spmd.clone.sunk | while | flops 3843487744 | bytes 27799436 | solution.py:86
  868.6 7.9 fusion.113
  914.8 26.4 %all-to-all-done.4 = bf16[8,512,256]{2,1,0:T(8,128)(2,1)S(1)} async-done(((bf16[8,512,256]{2,1,0:T(8,128)(2,1)}), bf16[8,512,256]{2,1,0:T(8,128)(2,1)S(1)}, u32[]{:S(2)}, u32[]{:S(2)}) %all-to-all-start.4) | async-done | bytes 2097184 | tf_op jit(solution)/shard_map/all_to_all | solution.py:203
  942.9 12.1 multiply_reduce_fusion.6
  963.5 10.2 fusion.117
  975.5 78.7 %reduce-scatter.11.cloned.1.call-done = f32[512,1024]{1,0:T(8,128)} async-done(((f32[2048,1024]{1,0:T(8,128)}), f32[512,1024]{1,0:T(8,128)}) %reduce-scatter.11.cloned.1.call-update) | async-done | bytes 2097168 | tf_op jit(solution)/shard_map/reduce_scatter | solution.py:258
  1054.2 302.1 %reduce-scatter.9.cloned.1.call-done = f32[256,4384]{0,1:T(8,128)} async-done(((f32[1024,4384]{0,1:T(8,128)}), f32[256,4384]{0,1:T(8,128)}) %reduce-scatter.9.cloned.1.call-update) | async-done | bytes 4489232 | tf_op jit(solution)/shard_map/reduce_scatter | solution.py:257
  1366.6 11.8 fusion.105
  1378.3 19.2 %all-reduce.23 = (f32[2304]{0:T(1024)S(1)}, f32[32]{0:T(128)S(1)}, f32[32]{0:T(128)S(1)}, f32[32]{0:T(128)S(1)}, f32[1024]{0:T(1024)S(1)}, /*index=5*/f32[2048]{0:T(1024)S(1)}) all-reduce(f32[2304]{0:T(1024)S(1)} %get-tuple-element.684, f32[32]{0:T(128)S(1)} %dynamic_update_slice.61, ...), channel_id=6, replica_groups=mesh['seq'=8,'wsh'=4] {'wsh'}, use_global_device_ids=true, to_apply=%region_35.36.clone | all-reduce | flops 5472 | bytes 43776
  1402.6 24.6 %all-reduce.21 = (f32[4,576]{1,0:T(4,128)}, f32[576]{0:T(1024)}, f32[8]{0:T(128)}, f32[8]{0:T(128)}, f32[8]{0:T(128)}, /*index=5*/f32[256]{0:T(256)}, f32[512]{0:T(512)}) all-reduce(f32[4,576]{1,0:T(4,128)S(1)} %copy.143, f32[576]{0:T(1024)S(1)} %dynamic-slice.5, f32[8]{0:T(128)S(1)} %dynamic-slice.7, ...), channel_id=1, replica_groups=mesh['seq'=8,'wsh'=4] {'seq'}, use_global_device_ids=true, to_apply=%region_31.32 | all-reduce | flops 3672 | bytes 29376 | tf_op jit(solution)/shard_map/psum | solution.py:242
  1427.2 72.2 %all-reduce.27.cloned.1.call-done = (f32[256,4384]{0,1:T(8,128)}, f32[512,1024]{1,0:T(8,128)}) async-done(((f32[256,4384]{0,1:T(8,128)}, f32[512,1024]{1,0:T(8,128)}), (f32[256,4384]{0,1:T(8,128)}, f32[512,1024]{1,0:T(8,128)})) %all-reduce.27.cloned.1.call-update) | async-done | bytes 6586384 | tf_op jit(solution)/shard_map/psum | solution.py:242
  (942 shorter events, 649.8 us)
Async XLA Ops:
  7.2 164.1 %all-gather.7.cloned.1.call-start = ((), (), s32[]{:S(2)}) async-start(), calls=%async_computation.10 | async-start | bytes 11223040 | tf_op jit(solution)/shard_map/all_gather | solution.py:106
  7.9 250.6 %all-gather.9.cloned.1.call-start = ((), (), s32[]{:S(2)}) async-start(), calls=%async_computation.11 | async-start | bytes 2359296 | tf_op jit(solution)/shard_map/all_gather | solution.py:153
  21.3 159.3 %copy-start.47 = (f32[4,1,256]{2,1,0:T(1,128)}, f32[4,1,256]{2,1,0:T(1,128)S(1)}, u32[]{:S(2)}) copy-start(f32[4,1,256]{2,1,0:T(1,128)S(1)} %convert_element_type.247) | copy-start | bytes 12292
  64.4 116.2 %copy-start.51 = (f32[512]{0:T(512)}, f32[512]{0:T(512)S(1)}, u32[]{:S(2)}) copy-start(f32[512]{0:T(512)S(1)} %fusion.140) | copy-start | bytes 6148
  64.4 132.9 %copy-start.37 = (f32[512]{0:T(512)}, f32[512]{0:T(512)S(1)}, u32[]{:S(2)}) copy-start(f32[512]{0:T(512)S(1)} %get-tuple-element.800) | copy-start | bytes 6148
  64.4 132.9 %copy-start.39 = (f32[512]{0:T(512)}, f32[512]{0:T(512)S(1)}, u32[]{:S(2)}) copy-start(f32[512]{0:T(512)S(1)} %get-tuple-element.801) | copy-start | bytes 6148
  64.5 132.9 %copy-start.41 = (f32[512]{0:T(512)}, f32[512]{0:T(512)S(1)}, u32[]{:S(2)}) copy-start(f32[512]{0:T(512)S(1)} %get-tuple-element.802) | copy-start | bytes 6148
  182.8 14.0 collective-permute-start
  204.3 9.6 all-to-all-start
  213.9 39.5 %copy-start.19 = (bf16[512,8,4]{0,2,1:T(4,128)(2,1)}, bf16[512,8,4]{0,2,1:T(4,128)(2,1)S(1)}, u32[]{:S(2)}) copy-start(bf16[512,8,4]{0,2,1:T(4,128)(2,1)S(1)} %all-to-all-done) | copy-start | bytes 98308
  213.9 36.4 %all-to-all-start.1 = ((bf16[8,512,256]{2,1,0:T(8,128)(2,1)}), bf16[8,512,256]{2,1,0:T(8,128)(2,1)S(1)}, u32[]{:S(2)}, u32[]{:S(2)}) async-start(bf16[8,512,256]{2,1,0:T(8,128)(2,1)} %fusion.121), calls=%async_computation.1 | async-start | bytes 4194304 | tf_op jit(solution)/shard_map/all_to_all | solution.py:148
  218.1 251.5 %all-gather.11.cloned.1.call-start = ((), (), s32[]{:S(2)}) async-start(), calls=%async_computation.12 | async-start | bytes 5242880 | tf_op jit(solution)/shard_map/all_gather | solution.py:107
  220.4 208.1 %copy-start.49 = (f32[256]{0:T(256)}, f32[256]{0:T(256)S(1)}, u32[]{:S(2)}) copy-start(f32[256]{0:T(256)S(1)} %mul.797) | copy-start | bytes 3076
  250.3 178.2 %copy-start.4 = (bf16[8,512,256]{2,1,0:T(8,128)(2,1)}, bf16[8,512,256]{2,1,0:T(8,128)(2,1)S(1)}, u32[]{:S(2)}) copy-start(bf16[8,512,256]{2,1,0:T(8,128)(2,1)S(1)} %all-to-all-done.1) | copy-start | bytes 6291460
  432.5 30.3 %all-to-all-start.2 = ((bf16[8,512,256]{2,1,0:T(8,128)(2,1)}), bf16[8,512,256]{2,1,0:T(8,128)(2,1)S(1)}, u32[]{:S(2)}, u32[]{:S(2)}) async-start(bf16[8,512,256]{2,1,0:T(8,128)(2,1)} %add_convert_fusion.1), calls=%async_computation.2 | async-start | bytes 4194304 | tf_op jit(solution)/shard_map/all_to_all | solution.py:175
  483.7 30.2 %all-to-all-start.3 = ((bf16[512,8,256]{2,0,1:T(8,128)(2,1)}), bf16[512,8,256]{2,0,1:T(8,128)(2,1)S(1)}, u32[]{:S(2)}, u32[]{:S(2)}) async-start(bf16[512,8,256]{2,0,1:T(8,128)(2,1)} %bitcast.441), calls=%async_computation.3 | async-start | bytes 4194304 | tf_op jit(solution)/shard_map/all_to_all | solution.py:196
  487.3 455.5 %reduce-scatter.7.cloned.1.call-start = ((), (), s32[]{:S(2)}) async-start(), calls=%async_computation.13 | async-start | bytes 2359296 | tf_op jit(solution)/shard_map/reduce_scatter | solution.py:210
  868.5 185.7 %reduce-scatter.11.cloned.1.call-start = ((), (), s32[]{:S(2)}) async-start(), calls=%async_computation.15 | async-start | bytes 10485760 | tf_op jit(solution)/shard_map/reduce_scatter | solution.py:258
  895.0 15.5 %all-to-all-start.5 = ((bf16[8,512,4]{1,2,0:T(4,128)(2,1)}), bf16[8,512,4]{1,2,0:T(4,128)(2,1)S(1)}, u32[]{:S(2)}, u32[]{:S(2)}) async-start(bf16[8,512,4]{1,2,0:T(4,128)(2,1)} %get-tuple-element.759), calls=%async_computation.6 | async-start | bytes 65536 | tf_op jit(solution)/shard_map/all_to_all | solution.py:206
  910.5 30.7 %all-to-all-start.4 = ((bf16[8,512,256]{2,1,0:T(8,128)(2,1)}), bf16[8,512,256]{2,1,0:T(8,128)(2,1)S(1)}, u32[]{:S(2)}, u32[]{:S(2)}) async-start(bf16[8,512,256]{2,1,0:T(8,128)(2,1)} %get-tuple-element.796), calls=%async_computation.4 | async-start | bytes 4194304 | tf_op jit(solution)/shard_map/all_to_all | solution.py:203
  914.6 441.7 %reduce-scatter.9.cloned.1.call-start = ((), (), s32[]{:S(2)}) async-start(), calls=%async_computation.14 | async-start | bytes 22446080 | tf_op jit(solution)/shard_map/reduce_scatter | solution.py:257
  957.0 3.8 collective-permute-start.1
  973.8 427.7 %reduce-scatter.13.cloned.1.call-start = ((), (), s32[]{:S(2)}) async-start(), calls=%async_computation.16 | async-start | bytes 1474560
  975.4 524.1 %all-reduce.27.cloned.1.call-start = ((), (), s32[]{:S(2)}) async-start(), calls=%async_computation.17 | async-start | bytes 13172736 | tf_op jit(solution)/shard_map/psum | solution.py:242
  (134 other events, 1317.5 us)
Sparse Core Ops, SparseCore 0:
  9.5 161.6 all-gather.6
  203.7 38.3 all-gather.8
  243.6 79.8 all-gather.10
  868.7 38.6 reduce-scatter.6
  909.5 144.6 reduce-scatter.10
  1056.4 299.8 reduce-scatter.8
  1358.6 30.4 reduce-scatter.12
  1392.6 106.8 all-reduce.26
